TPU v7x, 256 devices: a whole 4x4x8 slice. The times are simulated.
256 devices in a mesh: gx: 8 (over y, core), gy: 32 (over z, x).
Axes of the slice: x: 4, y: 4, z: 8, core: 2. Of those that a mesh axis runs over, the one named last changes fastest.
Arguments:
- right_side: float32 [256, 512, 256], P('gx', 'gy'), may hold values from -8 to 8
- coefficient: float32 [256, 512, 256], P('gx', 'gy'), may hold values from 0.1 to 10
Outputs:
- solution_field: float32 [256, 512, 256], P('gx', 'gy')
- residual: float32 [256, 512, 256], P('gx', 'gy')
All inputs are finite; a program needn't handle non-finite values.
Results may differ from a plain program's by a relative error of at most 0.0003.
Values sent between devices are 32-bit elements; how exact they have to be, the bound alone decides.
A program may use at most 128 MiB of HBM per device.

v0:
```python
from functools import partial
import jax
import jax.numpy as jnp
from jax import lax
from jax.sharding import PartitionSpec as P

LEVELS = 5
PRE = 2
POST = 2
BOTTOM = 8
SMOOTH_LO = 0.5
SMOOTH_HI = 2.0
COARSE_LO = 0.05
COARSE_HI = 2.0


def with_halo(value, sides, width):
    for axis, dim in sides:
        size, length = (lax.axis_size(axis), value.shape[dim])
        up = [(i, (i + 1) % size) for i in range(size - 1)]
        down = [(j, i) for i, j in up]
        last = lax.slice_in_dim(value, length - width, length, axis=dim)
        leading = lax.slice_in_dim(value, 0, width, axis=dim)
        before = lax.ppermute(last, axis, up)
        after = lax.ppermute(leading, axis, down)
        value = jnp.concatenate([before, value, after], axis=dim)
    return value


def harmonic(own, other):
    return 2.0 * own * other / (own + other)


def face_weights(conduct, padded):
    lower_x = jnp.where(padded[:-2, 1:-1, :] > 0.0, padded[:-2, 1:-1, :], conduct)
    upper_x = jnp.where(padded[2:, 1:-1, :] > 0.0, padded[2:, 1:-1, :], conduct)
    lower_y = jnp.where(padded[1:-1, :-2, :] > 0.0, padded[1:-1, :-2, :], conduct)
    upper_y = jnp.where(padded[1:-1, 2:, :] > 0.0, padded[1:-1, 2:, :], conduct)
    edged = jnp.pad(conduct, ((0, 0), (0, 0), (1, 1)), mode="edge")
    lower_z = edged[:, :, :-2]
    upper_z = edged[:, :, 2:]
    faces = [
        harmonic(conduct, other) for other in (lower_x, upper_x, lower_y, upper_y, lower_z, upper_z)
    ]
    total = faces[0] + faces[1] + faces[2] + faces[3] + faces[4] + faces[5]
    return tuple(faces) + (total,)


def stencil(field, padded, weights, scale):
    zpad = jnp.pad(field, ((0, 0), (0, 0), (1, 1)))
    beside = weights[0] * padded[:-2, 1:-1, :] + weights[1] * padded[2:, 1:-1, :]
    beside = beside + weights[2] * padded[1:-1, :-2, :] + weights[3] * padded[1:-1, 2:, :]
    beside = beside + weights[4] * zpad[:, :, :-2] + weights[5] * zpad[:, :, 2:]
    return scale * (weights[6] * field - beside)


def pad_plane(field):
    return jnp.pad(field, ((1, 1), (1, 1), (0, 0)))


def whole_operate(field, weights, scale):
    return stencil(field, pad_plane(field), weights, scale)


def local_operate(field, weights, scale):
    padded = with_halo(field, (("gx", 0), ("gy", 1)), 1)
    return stencil(field, padded, weights, scale)


def chebyshev(source, start, sweeps, low_end, high_end, operate, inverse):
    theta_val = (high_end + low_end) / 2.0
    half_width = (high_end - low_end) / 2.0
    sigma_val = theta_val / half_width
    rho_now = 1.0 / sigma_val
    if start is None:
        update = inverse * source / theta_val
        iterate = update
    else:
        update = inverse * (source - operate(start)) / theta_val
        iterate = start + update
    for sweep_index in range(sweeps - 1):
        rho_next = 1.0 / (2.0 * sigma_val - rho_now)
        update = rho_next * rho_now * update + 2.0 * rho_next / half_width * inverse * (
            source - operate(iterate)
        )
        iterate = iterate + update
        rho_now = rho_next
    return iterate


def restrict(field):
    size_x, size_y, size_z = field.shape
    return jnp.mean(field.reshape(size_x // 2, 2, size_y // 2, 2, size_z // 2, 2), axis=(1, 3, 5))


def prolong(field):
    size_x, size_y, size_z = field.shape
    grown = jnp.broadcast_to(field[:, None, :, None, :, None], (size_x, 2, size_y, 2, size_z, 2))
    return grown.reshape(2 * size_x, 2 * size_y, 2 * size_z)


def cycle(level_index, source, conduct):
    weights = face_weights(conduct, pad_plane(conduct))
    scale = 0.25**level_index
    inverse = 1.0 / (scale * weights[6])
    operate = partial(whole_operate, weights=weights, scale=scale)
    return chebyshev(source, None, BOTTOM, COARSE_LO, COARSE_HI, operate, inverse)


def collect(source, conduct):
    block_x, block_y, block_z = source.shape
    count_x = lax.axis_size("gx")
    count_y = lax.axis_size("gy")
    gathered = (
        lax.all_gather(source, ("gx", "gy"), axis=0, tiled=True),
        lax.all_gather(conduct, ("gx", "gy"), axis=0, tiled=True),
    )
    arranged = []
    for member in gathered:
        blocks = member.reshape(count_x, count_y, block_x, block_y, block_z)
        arranged.append(
            blocks.transpose(0, 2, 1, 3, 4).reshape(count_x * block_x, count_y * block_y, block_z)
        )
    return (arranged[0], arranged[1])


def own_block(whole, shape):
    start_x = lax.axis_index("gx") * shape[0]
    start_y = lax.axis_index("gy") * shape[1]
    return lax.dynamic_slice(whole, (start_x, start_y, jnp.zeros((), jnp.int32)), shape)


def per_device(right_side, coefficient):
    joined = LEVELS - 1
    conducts = [coefficient]
    for level_index in range(1, joined + 1):
        conducts.append(restrict(conducts[-1]))
    operators = []
    inverses = []
    for level_index in range(joined):
        padded = with_halo(conducts[level_index], (("gx", 0), ("gy", 1)), 1)
        weights = face_weights(conducts[level_index], padded)
        scale = 0.25**level_index
        inverses.append(1.0 / (scale * weights[6]))
        operators.append(partial(local_operate, weights=weights, scale=scale))
    sources = [right_side]
    smoothed = []
    for level_index in range(joined):
        operate = operators[level_index]
        iterate = chebyshev(
            sources[level_index], None, PRE, SMOOTH_LO, SMOOTH_HI, operate, inverses[level_index]
        )
        smoothed.append(iterate)
        sources.append(restrict(sources[level_index] - operate(iterate)))
    whole_source, whole_conduct = collect(sources[joined], conducts[joined])
    correction = own_block(cycle(joined, whole_source, whole_conduct), sources[joined].shape)
    for level_index in reversed(range(joined)):
        iterate = smoothed[level_index] + prolong(correction)
        correction = chebyshev(
            sources[level_index],
            iterate,
            POST,
            SMOOTH_LO,
            SMOOTH_HI,
            operators[level_index],
            inverses[level_index],
        )
    residual = right_side - operators[0](correction)
    return (correction, residual)


def solution(mesh):
    in_specs = (P("gx", "gy", None), P("gx", "gy", None))
    out_specs = (P("gx", "gy", None), P("gx", "gy", None))
    return jax.shard_map(
        per_device, mesh=mesh, in_specs=in_specs, out_specs=out_specs, check_vma=False
    )
```

profile of v0, /device:TPU:103, one launch (start us, length us, event | category | flops | bytes accessed | tf_op | source)
XLA Modules:
  0.0 702.0 jit_solution(18021534122502074643)
XLA Ops:
  1.4 3.8 collective-permute-start
  7.2 35.6 %reshape.80 = f32[16,2,8,2,128,2]{5,4,3,2,1,0:T(8,128)} reshape(f32[32,16,256]{2,1,0:T(8,128)} %param.3) | data formatting | bytes 1048576 | tf_op jit(solution)/shard_map/reshape | solution.py:93
  42.8 12.2 %reduce_sum.86 = f32[16,8,128]{2,1,0:T(8,128)S(1)} reduce(f32[16,2,8,2,128,2]{5,4,3,2,1,0:T(8,128)} %reshape.80, f32[]{:T(128)} %constant.35.clone.1), dimensions={1,3,5}, to_apply=%region_0.0 | reduce | flops 114688 | bytes 589828 | tf_op jit(solution)/shard_map/reduce_sum | solution.py:93
  55.6 3.6 collective-permute-start.8
  62.0 5.5 div.203
  70.2 4.7 collective-permute-start.2
  76.9 6.0 collective-permute-done.3
  84.8 5.1 collective-permute-start.4
  92.4 3.6 collective-permute-start.20
  98.1 3.4 collective-permute-start.7
  106.3 3.8 fusion.7
  124.2 6.5 collective-permute-start.10
  134.1 35.6 %reshape.81 = f32[16,2,8,2,128,2]{5,4,3,2,1,0:T(8,128)} reshape(f32[32,16,256]{2,1,0:T(8,128)} %fusion.13) | data formatting | bytes 1048576 | tf_op jit(solution)/shard_map/reshape | solution.py:93
  169.7 12.2 %reduce_sum.87 = f32[16,8,128]{2,1,0:T(8,128)S(1)} reduce(f32[16,2,8,2,128,2]{5,4,3,2,1,0:T(8,128)} %reshape.81, f32[]{:T(128)} %constant.35.clone.1), dimensions={1,3,5}, to_apply=%region_1.0 | reduce | flops 114688 | bytes 589828 | tf_op jit(solution)/shard_map/reduce_sum | solution.py:93
  183.7 4.5 collective-permute-start.16
  191.5 3.6 collective-permute-start.32
  195.1 7.0 collective-permute-start.18
  205.5 4.7 collective-permute-done.19
  229.5 5.3 collective-permute-start.22
  238.6 6.3 reshape.82
  249.2 4.5 collective-permute-start.28
  258.6 7.0 collective-permute-start.30
  267.5 59.7 %all-gather.2 = f32[256,2,16]{2,1,0:T(2,128)S(1)} all-gather(f32[1,2,16]{2,1,0:T(2,128)S(1)} %multiply_bitcast_fusion.1), channel_id=2, replica_groups=mesh['gx'=8,'gy'=32] {'gx','gy'}, dimensions={0}, use_global_device_ids=true | all-gather | bytes 32896 | tf_op jit(solution)/shard_map/all_gather | solution.py:116
  328.2 4.6 collective-permute-start.36
  343.7 6.0 collective-permute-start.34
  358.8 3.9 collective-permute-start.40
  367.6 5.1 collective-permute-start.42
  374.7 3.8 multiply_divide_fusion
  381.7 3.4 collective-permute-start.44
  391.5 3.9 collective-permute-start.46
  397.4 6.0 collective-permute-done.47
  408.4 57.4 %all-gather.3 = f32[256,2,16]{2,1,0:T(2,128)S(1)} all-gather(f32[1,2,16]{2,1,0:T(2,128)S(1)} %multiply_bitcast_fusion), channel_id=3, replica_groups=mesh['gx'=8,'gy'=32] {'gx','gy'}, dimensions={0}, use_global_device_ids=true | all-gather | bytes 32896 | tf_op jit(solution)/shard_map/all_gather | solution.py:115
  479.7 4.6 collective-permute-start.48
  489.3 5.3 collective-permute-start.50
  496.5 5.8 collective-permute-done.51
  513.2 3.4 collective-permute-start.55
  516.6 4.3 collective-permute-done.55
  538.0 4.3 collective-permute-done.59
  556.5 4.3 collective-permute-done.63
  564.4 4.0 reshape.89
  582.6 4.6 collective-permute-done.67
  601.6 4.3 collective-permute-done.71
  607.1 11.4 %broadcast_in_dim.36 = f32[16,2,8,2,128,2]{5,4,3,2,1,0:T(8,128)} broadcast(f32[16,8,128]{2,1,0:T(8,128)S(1)} %fusion.220), dimensions={0,2,4} | broadcast | bytes 589824 | tf_op jit(solution)/shard_map/broadcast_in_dim | solution.py:98
  618.5 24.6 %reshape.90 = f32[32,16,256]{2,1,0:T(8,128)} reshape(f32[16,2,8,2,128,2]{5,4,3,2,1,0:T(8,128)} %broadcast_in_dim.36) | data formatting | bytes 1048576 | tf_op jit(solution)/shard_map/reshape | solution.py:99
  654.5 3.4 collective-permute-start.75
  657.9 4.6 collective-permute-done.75
  676.9 4.6 collective-permute-done.79
  695.9 4.6 collective-permute-done.83
  (313 shorter events, 263.2 us)
Async XLA Ops:
  1.4 68.7 %collective-permute-start = (f32[1,16,256]{2,1,0:T(8,128)S(1)}, f32[1,16,256]{2,1,0:T(8,128)S(1)}, u32[]{:S(2)}, u32[]{:S(2)}) collective-permute-start(f32[1,16,256]{2,1,0:T(8,128)S(1)} %get-tuple-element.81), channel_id=1, source_target_pairs={{0,32},{32,64},{64,96},{96,128},{128,160},{160,192},{192,224},{1,3... | collective-permute-start | bytes 49160 | tf_op jit(solution)/shard_map/ppermute | solution.py:24
  5.2 65.0 %collective-permute-start.1 = (f32[1,16,256]{2,1,0:T(8,128)S(1)}, f32[1,16,256]{2,1,0:T(8,128)S(1)}, u32[]{:S(2)}, u32[]{:S(2)}) collective-permute-start(f32[1,16,256]{2,1,0:T(8,128)S(1)} %get-tuple-element.80), channel_id=1, source_target_pairs={{32,0},{64,32},{96,64},{128,96},{160,128},{192,160},{224,192},{33,... | collective-permute-start | bytes 49160 | tf_op jit(solution)/shard_map/ppermute | solution.py:25
  55.6 65.6 %collective-permute-start.8 = (f32[1,8,128]{2,1,0:T(8,128)}, f32[1,8,128]{2,1,0:T(8,128)}, u32[]{:S(2)}, u32[]{:S(2)}) collective-permute-start(f32[1,8,128]{2,1,0:T(8,128)} %get-tuple-element.104), channel_id=1, source_target_pairs={{0,32},{32,64},{64,96},{96,128},{128,160},{160,192},{192,224},{1,3... | collective-permute-start | bytes 12296 | tf_op jit(solution)/shard_map/ppermute | solution.py:24
  59.3 64.1 %collective-permute-start.9 = (f32[1,8,128]{2,1,0:T(8,128)}, f32[1,8,128]{2,1,0:T(8,128)}, u32[]{:S(2)}, u32[]{:S(2)}) collective-permute-start(f32[1,8,128]{2,1,0:T(8,128)} %get-tuple-element.105), channel_id=1, source_target_pairs={{32,0},{64,32},{96,64},{128,96},{160,128},{192,160},{224,192},{33,... | collective-permute-start | bytes 12296 | tf_op jit(solution)/shard_map/ppermute | solution.py:25
  74.9 8.0 %collective-permute-start.3 = (f32[34,1,256]{2,1,0:T(1,128)S(1)}, f32[34,1,256]{2,1,0:T(1,128)S(1)}, u32[]{:S(2)}, u32[]{:S(2)}) collective-permute-start(f32[34,1,256]{2,1,0:T(1,128)S(1)} %get-tuple-element.66), channel_id=1, source_target_pairs={{1,0},{2,1},{3,2},{4,3},{5,4},{6,5},{7,6},{8,7},{9,8},{10,9},{11,1... | collective-permute-start | bytes 104456 | tf_op jit(solution)/shard_map/ppermute | solution.py:25
  84.8 11.2 %collective-permute-start.4 = (f32[1,16,256]{2,1,0:T(8,128)S(1)}, f32[1,16,256]{2,1,0:T(8,128)S(1)}, u32[]{:S(2)}, u32[]{:S(2)}) collective-permute-start(f32[1,16,256]{2,1,0:T(8,128)S(1)} %get-tuple-element.76), channel_id=1, source_target_pairs={{0,32},{32,64},{64,96},{96,128},{128,160},{160,192},{192,224},{1,3... | collective-permute-start | bytes 49160 | tf_op jit(solution)/shard_map/ppermute | solution.py:24
  92.4 132.4 %collective-permute-start.20 = (f32[1,4,64]{2,1,0:T(4,128)}, f32[1,4,64]{2,1,0:T(4,128)}, u32[]{:S(2)}, u32[]{:S(2)}) collective-permute-start(f32[1,4,64]{2,1,0:T(4,128)} %get-tuple-element.126), channel_id=1, source_target_pairs={{0,32},{32,64},{64,96},{96,128},{128,160},{160,192},{192,224},{1,3... | collective-permute-start | bytes 3080 | tf_op jit(solution)/shard_map/ppermute | solution.py:24
  96.1 8.5 %collective-permute-start.6 = (f32[34,1,256]{2,1,0:T(1,128)S(1)}, f32[34,1,256]{2,1,0:T(1,128)S(1)}, u32[]{:S(2)}, u32[]{:S(2)}) collective-permute-start(f32[34,1,256]{2,1,0:T(1,128)S(1)} %get-tuple-element.64), channel_id=1, source_target_pairs={{0,1},{1,2},{2,3},{3,4},{4,5},{5,6},{6,7},{7,8},{8,9},{9,10},{10,1... | collective-permute-start | bytes 104456 | tf_op jit(solution)/shard_map/ppermute | solution.py:24
  98.1 8.3 %collective-permute-start.7 = (f32[34,1,256]{2,1,0:T(1,128)S(1)}, f32[34,1,256]{2,1,0:T(1,128)S(1)}, u32[]{:S(2)}, u32[]{:S(2)}) collective-permute-start(f32[34,1,256]{2,1,0:T(1,128)S(1)} %get-tuple-element.65), channel_id=1, source_target_pairs={{1,0},{2,1},{3,2},{4,3},{5,4},{6,5},{7,6},{8,7},{9,8},{10,9},{11,1... | collective-permute-start | bytes 104456 | tf_op jit(solution)/shard_map/ppermute | solution.py:25
  116.0 112.1 %collective-permute-start.21 = (f32[1,4,64]{2,1,0:T(4,128)}, f32[1,4,64]{2,1,0:T(4,128)}, u32[]{:S(2)}, u32[]{:S(2)}) collective-permute-start(f32[1,4,64]{2,1,0:T(4,128)} %get-tuple-element.127), channel_id=1, source_target_pairs={{32,0},{64,32},{96,64},{128,96},{160,128},{192,160},{224,192},{33,... | collective-permute-start | bytes 3080 | tf_op jit(solution)/shard_map/ppermute | solution.py:25
  118.1 12.6 %collective-permute-start.14 = (f32[34,1,256]{2,1,0:T(1,128)S(1)}, f32[34,1,256]{2,1,0:T(1,128)S(1)}, u32[]{:S(2)}, u32[]{:S(2)}) collective-permute-start(f32[34,1,256]{2,1,0:T(1,128)S(1)} %get-tuple-element.62), channel_id=1, source_target_pairs={{0,1},{1,2},{2,3},{3,4},{4,5},{5,6},{6,7},{7,8},{8,9},{9,10},{10,1... | collective-permute-start | bytes 104456 | tf_op jit(solution)/shard_map/ppermute | solution.py:24
  121.2 11.3 %collective-permute-start.15 = (f32[34,1,256]{2,1,0:T(1,128)S(1)}, f32[34,1,256]{2,1,0:T(1,128)S(1)}, u32[]{:S(2)}, u32[]{:S(2)}) collective-permute-start(f32[34,1,256]{2,1,0:T(1,128)S(1)} %get-tuple-element.63), channel_id=1, source_target_pairs={{1,0},{2,1},{3,2},{4,3},{5,4},{6,5},{7,6},{8,7},{9,8},{10,9},{11,1... | collective-permute-start | bytes 104456 | tf_op jit(solution)/shard_map/ppermute | solution.py:25
  124.2 57.8 %collective-permute-start.10 = (f32[18,1,128]{2,1,0:T(1,128)S(1)}, f32[18,1,128]{2,1,0:T(1,128)}, u32[]{:S(2)}, u32[]{:S(2)}) collective-permute-start(f32[18,1,128]{2,1,0:T(1,128)S(1)} %get-tuple-element.93), channel_id=1, source_target_pairs={{0,1},{1,2},{2,3},{3,4},{4,5},{5,6},{6,7},{7,8},{8,9},{9,10},{10,1... | collective-permute-start | bytes 27656 | tf_op jit(solution)/shard_map/ppermute | solution.py:24
  130.7 51.3 %collective-permute-start.11 = (f32[18,1,128]{2,1,0:T(1,128)S(1)}, f32[18,1,128]{2,1,0:T(1,128)S(1)}, u32[]{:S(2)}, u32[]{:S(2)}) collective-permute-start(f32[18,1,128]{2,1,0:T(1,128)S(1)} %get-tuple-element.92), channel_id=1, source_target_pairs={{1,0},{2,1},{3,2},{4,3},{5,4},{6,5},{7,6},{8,7},{9,8},{10,9},{11,1... | collective-permute-start | bytes 27656 | tf_op jit(solution)/shard_map/ppermute | solution.py:25
  183.7 11.4 %collective-permute-start.16 = (f32[1,8,128]{2,1,0:T(8,128)S(1)}, f32[1,8,128]{2,1,0:T(8,128)S(1)}, u32[]{:S(2)}, u32[]{:S(2)}) collective-permute-start(f32[1,8,128]{2,1,0:T(8,128)S(1)} %get-tuple-element.100), channel_id=1, source_target_pairs={{0,32},{32,64},{64,96},{96,128},{128,160},{160,192},{192,224},{1,3... | collective-permute-start | bytes 12296 | tf_op jit(solution)/shard_map/ppermute | solution.py:24
  188.2 6.9 collective-permute-start.17
  191.5 144.2 %collective-permute-start.32 = (f32[1,2,32]{2,0,1:T(1,128)}, f32[1,2,32]{2,0,1:T(1,128)}, u32[]{:S(2)}, u32[]{:S(2)}) collective-permute-start(f32[1,2,32]{2,0,1:T(1,128)} %get-tuple-element.150), channel_id=1, source_target_pairs={{0,32},{32,64},{64,96},{96,128},{128,160},{160,192},{192,224},{1,3... | collective-permute-start | bytes 776 | tf_op jit(solution)/shard_map/ppermute | solution.py:24
  195.1 10.4 %collective-permute-start.18 = (f32[18,1,128]{2,1,0:T(1,128)S(1)}, f32[18,1,128]{2,1,0:T(1,128)S(1)}, u32[]{:S(2)}, u32[]{:S(2)}) collective-permute-start(f32[18,1,128]{2,1,0:T(1,128)S(1)} %get-tuple-element.90), channel_id=1, source_target_pairs={{0,1},{1,2},{2,3},{3,4},{4,5},{5,6},{6,7},{7,8},{8,9},{9,10},{10,1... | collective-permute-start | bytes 27656 | tf_op jit(solution)/shard_map/ppermute | solution.py:24
  202.1 8.1 %collective-permute-start.19 = (f32[18,1,128]{2,1,0:T(1,128)S(1)}, f32[18,1,128]{2,1,0:T(1,128)S(1)}, u32[]{:S(2)}, u32[]{:S(2)}) collective-permute-start(f32[18,1,128]{2,1,0:T(1,128)S(1)} %get-tuple-element.91), channel_id=1, source_target_pairs={{1,0},{2,1},{3,2},{4,3},{5,4},{6,5},{7,6},{8,7},{9,8},{10,9},{11,1... | collective-permute-start | bytes 27656 | tf_op jit(solution)/shard_map/ppermute | solution.py:25
  211.0 9.1 %collective-permute-start.24 = (f32[1,8,128]{2,1,0:T(8,128)}, f32[1,8,128]{2,1,0:T(8,128)}, u32[]{:S(2)}, u32[]{:S(2)}) collective-permute-start(f32[1,8,128]{2,1,0:T(8,128)} %get-tuple-element.98), channel_id=1, source_target_pairs={{0,32},{32,64},{64,96},{96,128},{128,160},{160,192},{192,224},{1,3... | collective-permute-start | bytes 12296 | tf_op jit(solution)/shard_map/ppermute | solution.py:24
  214.0 8.1 %collective-permute-start.25 = (f32[1,8,128]{2,1,0:T(8,128)}, f32[1,8,128]{2,1,0:T(8,128)}, u32[]{:S(2)}, u32[]{:S(2)}) collective-permute-start(f32[1,8,128]{2,1,0:T(8,128)} %get-tuple-element.99), channel_id=1, source_target_pairs={{32,0},{64,32},{96,64},{128,96},{160,128},{192,160},{224,192},{33,... | collective-permute-start | bytes 12296 | tf_op jit(solution)/shard_map/ppermute | solution.py:25
  220.1 115.6 %collective-permute-start.33 = (f32[1,2,32]{2,0,1:T(1,128)}, f32[1,2,32]{2,0,1:T(1,128)}, u32[]{:S(2)}, u32[]{:S(2)}) collective-permute-start(f32[1,2,32]{2,0,1:T(1,128)} %get-tuple-element.151), channel_id=1, source_target_pairs={{32,0},{64,32},{96,64},{128,96},{160,128},{192,160},{224,192},{33,... | collective-permute-start | bytes 776 | tf_op jit(solution)/shard_map/ppermute | solution.py:25
  222.8 12.0 %collective-permute-start.26 = (f32[18,1,128]{2,1,0:T(1,128)S(1)}, f32[18,1,128]{2,1,0:T(1,128)S(1)}, u32[]{:S(2)}, u32[]{:S(2)}) collective-permute-start(f32[18,1,128]{2,1,0:T(1,128)S(1)} %get-tuple-element.88), channel_id=1, source_target_pairs={{0,1},{1,2},{2,3},{3,4},{4,5},{5,6},{6,7},{7,8},{8,9},{9,10},{10,1... | collective-permute-start | bytes 27656 | tf_op jit(solution)/shard_map/ppermute | solution.py:24
  224.8 12.1 %collective-permute-start.27 = (f32[18,1,128]{2,1,0:T(1,128)S(1)}, f32[18,1,128]{2,1,0:T(1,128)S(1)}, u32[]{:S(2)}, u32[]{:S(2)}) collective-permute-start(f32[18,1,128]{2,1,0:T(1,128)S(1)} %get-tuple-element.89), channel_id=1, source_target_pairs={{1,0},{2,1},{3,2},{4,3},{5,4},{6,5},{7,6},{8,7},{9,8},{10,9},{11,1... | collective-permute-start | bytes 27656 | tf_op jit(solution)/shard_map/ppermute | solution.py:25
  229.5 18.5 %collective-permute-start.22 = (f32[10,1,64]{2,1,0:T(1,128)}, f32[10,1,64]{2,1,0:T(1,128)}, u32[]{:S(2)}, u32[]{:S(2)}) collective-permute-start(f32[10,1,64]{2,1,0:T(1,128)} %get-tuple-element.115), channel_id=1, source_target_pairs={{0,1},{1,2},{2,3},{3,4},{4,5},{5,6},{6,7},{7,8},{8,9},{9,10},{10,1... | collective-permute-start | bytes 7688 | tf_op jit(solution)/shard_map/ppermute | solution.py:24
  234.8 13.2 %collective-permute-start.23 = (f32[10,1,64]{2,1,0:T(1,128)}, f32[10,1,64]{2,1,0:T(1,128)}, u32[]{:S(2)}, u32[]{:S(2)}) collective-permute-start(f32[10,1,64]{2,1,0:T(1,128)} %get-tuple-element.114), channel_id=1, source_target_pairs={{1,0},{2,1},{3,2},{4,3},{5,4},{6,5},{7,6},{8,7},{9,8},{10,9},{11,1... | collective-permute-start | bytes 7688 | tf_op jit(solution)/shard_map/ppermute | solution.py:25
  249.2 7.1 %collective-permute-start.28 = (f32[1,4,64]{2,1,0:T(4,128)S(1)}, f32[1,4,64]{2,1,0:T(4,128)S(1)}, u32[]{:S(2)}, u32[]{:S(2)}) collective-permute-start(f32[1,4,64]{2,1,0:T(4,128)S(1)} %get-tuple-element.122), channel_id=1, source_target_pairs={{0,32},{32,64},{64,96},{96,128},{128,160},{160,192},{192,224},{1,3... | collective-permute-start | bytes 3080 | tf_op jit(solution)/shard_map/ppermute | solution.py:24
  258.6 68.7 %collective-permute-start.30 = (f32[10,1,64]{2,1,0:T(1,128)S(1)}, f32[10,1,64]{2,1,0:T(1,128)S(1)}, u32[]{:S(2)}, u32[]{:S(2)}) collective-permute-start(f32[10,1,64]{2,1,0:T(1,128)S(1)} %get-tuple-element.112), channel_id=1, source_target_pairs={{0,1},{1,2},{2,3},{3,4},{4,5},{5,6},{6,7},{7,8},{8,9},{9,10},{10,1... | collective-permute-start | bytes 7688 | tf_op jit(solution)/shard_map/ppermute | solution.py:24
  265.6 61.8 %collective-permute-start.31 = (f32[10,1,64]{2,1,0:T(1,128)S(1)}, f32[10,1,64]{2,1,0:T(1,128)S(1)}, u32[]{:S(2)}, u32[]{:S(2)}) collective-permute-start(f32[10,1,64]{2,1,0:T(1,128)S(1)} %get-tuple-element.113), channel_id=1, source_target_pairs={{1,0},{2,1},{3,2},{4,3},{5,4},{6,5},{7,6},{8,7},{9,8},{10,9},{11,1... | collective-permute-start | bytes 7688 | tf_op jit(solution)/shard_map/ppermute | solution.py:25
  328.2 8.2 %collective-permute-start.36 = (f32[1,4,64]{2,1,0:T(4,128)S(1)}, f32[1,4,64]{2,1,0:T(4,128)S(1)}, u32[]{:S(2)}, u32[]{:S(2)}) collective-permute-start(f32[1,4,64]{2,1,0:T(4,128)S(1)} %get-tuple-element.120), channel_id=1, source_target_pairs={{0,32},{32,64},{64,96},{96,128},{128,160},{160,192},{192,224},{1,3... | collective-permute-start | bytes 3080 | tf_op jit(solution)/shard_map/ppermute | solution.py:24
  337.8 13.8 %collective-permute-start.38 = (f32[10,1,64]{2,1,0:T(1,128)S(1)}, f32[10,1,64]{2,1,0:T(1,128)S(1)}, u32[]{:S(2)}, u32[]{:S(2)}) collective-permute-start(f32[10,1,64]{2,1,0:T(1,128)S(1)} %get-tuple-element.110), channel_id=1, source_target_pairs={{0,1},{1,2},{2,3},{3,4},{4,5},{5,6},{6,7},{7,8},{8,9},{9,10},{10,1... | collective-permute-start | bytes 7688 | tf_op jit(solution)/shard_map/ppermute | solution.py:24
  340.5 11.1 %collective-permute-start.39 = (f32[10,1,64]{2,1,0:T(1,128)S(1)}, f32[10,1,64]{2,1,0:T(1,128)S(1)}, u32[]{:S(2)}, u32[]{:S(2)}) collective-permute-start(f32[10,1,64]{2,1,0:T(1,128)S(1)} %get-tuple-element.111), channel_id=1, source_target_pairs={{1,0},{2,1},{3,2},{4,3},{5,4},{6,5},{7,6},{8,7},{9,8},{10,9},{11,1... | collective-permute-start | bytes 7688 | tf_op jit(solution)/shard_map/ppermute | solution.py:25
  343.7 13.3 %collective-permute-start.34 = (f32[6,1,32]{2,0,1:T(8,128)}, f32[6,1,32]{2,0,1:T(8,128)}, u32[]{:S(2)}, u32[]{:S(2)}) collective-permute-start(f32[6,1,32]{2,0,1:T(8,128)} %get-tuple-element.137), channel_id=1, source_target_pairs={{0,1},{1,2},{2,3},{3,4},{4,5},{5,6},{6,7},{7,8},{8,9},{9,10},{10,1... | collective-permute-start | bytes 2312 | tf_op jit(solution)/shard_map/ppermute | solution.py:24
  349.7 8.0 %collective-permute-start.35 = (f32[6,1,32]{2,0,1:T(8,128)}, f32[6,1,32]{2,0,1:T(8,128)}, u32[]{:S(2)}, u32[]{:S(2)}) collective-permute-start(f32[6,1,32]{2,0,1:T(8,128)} %get-tuple-element.136), channel_id=1, source_target_pairs={{1,0},{2,1},{3,2},{4,3},{5,4},{6,5},{7,6},{8,7},{9,8},{10,9},{11,1... | collective-permute-start | bytes 2312 | tf_op jit(solution)/shard_map/ppermute | solution.py:25
  367.6 10.9 %collective-permute-start.42 = (f32[6,1,32]{2,0,1:T(8,128)S(1)}, f32[6,1,32]{2,0,1:T(8,128)S(1)}, u32[]{:S(2)}, u32[]{:S(2)}) collective-permute-start(f32[6,1,32]{2,0,1:T(8,128)S(1)} %get-tuple-element.134), channel_id=1, source_target_pairs={{0,1},{1,2},{2,3},{3,4},{4,5},{5,6},{6,7},{7,8},{8,9},{9,10},{10,1... | collective-permute-start | bytes 2312 | tf_op jit(solution)/shard_map/ppermute | solution.py:24
  372.7 7.7 %collective-permute-start.43 = (f32[6,1,32]{2,0,1:T(8,128)S(1)}, f32[6,1,32]{2,0,1:T(8,128)S(1)}, u32[]{:S(2)}, u32[]{:S(2)}) collective-permute-start(f32[6,1,32]{2,0,1:T(8,128)S(1)} %get-tuple-element.135), channel_id=1, source_target_pairs={{1,0},{2,1},{3,2},{4,3},{5,4},{6,5},{7,6},{8,7},{9,8},{10,9},{11,1... | collective-permute-start | bytes 2312 | tf_op jit(solution)/shard_map/ppermute | solution.py:25
  395.4 8.0 %collective-permute-start.47 = (f32[6,1,32]{2,0,1:T(8,128)}, f32[6,1,32]{2,0,1:T(8,128)}, u32[]{:S(2)}, u32[]{:S(2)}) collective-permute-start(f32[6,1,32]{2,0,1:T(8,128)} %get-tuple-element.133), channel_id=1, source_target_pairs={{1,0},{2,1},{3,2},{4,3},{5,4},{6,5},{7,6},{8,7},{9,8},{10,9},{11,1... | collective-permute-start | bytes 2312 | tf_op jit(solution)/shard_map/ppermute | solution.py:25
  479.7 7.3 %collective-permute-start.48 = (f32[1,2,32]{2,0,1:T(1,128)S(1)}, f32[1,2,32]{2,0,1:T(1,128)S(1)}, u32[]{:S(2)}, u32[]{:S(2)}) collective-permute-start(f32[1,2,32]{2,0,1:T(1,128)S(1)} %get-tuple-element.140), channel_id=1, source_target_pairs={{0,32},{32,64},{64,96},{96,128},{128,160},{160,192},{192,224},{1,3... | collective-permute-start | bytes 776 | tf_op jit(solution)/shard_map/ppermute | solution.py:24
  489.3 7.2 %collective-permute-start.50 = (f32[6,1,32]{2,0,1:T(8,128)S(1)}, f32[6,1,32]{2,0,1:T(8,128)S(1)}, u32[]{:S(2)}, u32[]{:S(2)}) collective-permute-start(f32[6,1,32]{2,0,1:T(8,128)S(1)} %get-tuple-element.130), channel_id=1, source_target_pairs={{0,1},{1,2},{2,3},{3,4},{4,5},{5,6},{6,7},{7,8},{8,9},{9,10},{10,1... | collective-permute-start | bytes 2312 | tf_op jit(solution)/shard_map/ppermute | solution.py:24
  494.5 7.7 %collective-permute-start.51 = (f32[6,1,32]{2,0,1:T(8,128)S(1)}, f32[6,1,32]{2,0,1:T(8,128)S(1)}, u32[]{:S(2)}, u32[]{:S(2)}) collective-permute-start(f32[6,1,32]{2,0,1:T(8,128)S(1)} %get-tuple-element.131), channel_id=1, source_target_pairs={{1,0},{2,1},{3,2},{4,3},{5,4},{6,5},{7,6},{8,7},{9,8},{10,9},{11,1... | collective-permute-start | bytes 2312 | tf_op jit(solution)/shard_map/ppermute | solution.py:25
  513.2 7.7 %collective-permute-start.55 = (f32[6,1,32]{2,0,1:T(8,128)S(1)}, f32[6,1,32]{2,0,1:T(8,128)S(1)}, u32[]{:S(2)}, u32[]{:S(2)}) collective-permute-start(f32[6,1,32]{2,0,1:T(8,128)S(1)} %get-tuple-element.129), channel_id=1, source_target_pairs={{1,0},{2,1},{3,2},{4,3},{5,4},{6,5},{7,6},{8,7},{9,8},{10,9},{11,1... | collective-permute-start | bytes 2312 | tf_op jit(solution)/shard_map/ppermute | solution.py:25
  534.6 7.7 %collective-permute-start.59 = (f32[10,1,64]{2,1,0:T(1,128)S(1)}, f32[10,1,64]{2,1,0:T(1,128)S(1)}, u32[]{:S(2)}, u32[]{:S(2)}) collective-permute-start(f32[10,1,64]{2,1,0:T(1,128)S(1)} %get-tuple-element.109), channel_id=1, source_target_pairs={{1,0},{2,1},{3,2},{4,3},{5,4},{6,5},{7,6},{8,7},{9,8},{10,9},{11,1... | collective-permute-start | bytes 7688 | tf_op jit(solution)/shard_map/ppermute | solution.py:25
  553.2 7.7 %collective-permute-start.63 = (f32[10,1,64]{2,1,0:T(1,128)S(1)}, f32[10,1,64]{2,1,0:T(1,128)S(1)}, u32[]{:S(2)}, u32[]{:S(2)}) collective-permute-start(f32[10,1,64]{2,1,0:T(1,128)S(1)} %get-tuple-element.107), channel_id=1, source_target_pairs={{1,0},{2,1},{3,2},{4,3},{5,4},{6,5},{7,6},{8,7},{9,8},{10,9},{11,1... | collective-permute-start | bytes 7688 | tf_op jit(solution)/shard_map/ppermute | solution.py:25
  579.5 7.7 %collective-permute-start.67 = (f32[18,1,128]{2,1,0:T(1,128)S(1)}, f32[18,1,128]{2,1,0:T(1,128)S(1)}, u32[]{:S(2)}, u32[]{:S(2)}) collective-permute-start(f32[18,1,128]{2,1,0:T(1,128)S(1)} %get-tuple-element.87), channel_id=1, source_target_pairs={{1,0},{2,1},{3,2},{4,3},{5,4},{6,5},{7,6},{8,7},{9,8},{10,9},{11,1... | collective-permute-start | bytes 27656 | tf_op jit(solution)/shard_map/ppermute | solution.py:25
  598.3 7.7 %collective-permute-start.71 = (f32[18,1,128]{2,1,0:T(1,128)S(1)}, f32[18,1,128]{2,1,0:T(1,128)S(1)}, u32[]{:S(2)}, u32[]{:S(2)}) collective-permute-start(f32[18,1,128]{2,1,0:T(1,128)S(1)} %get-tuple-element.85), channel_id=1, source_target_pairs={{1,0},{2,1},{3,2},{4,3},{5,4},{6,5},{7,6},{8,7},{9,8},{10,9},{11,1... | collective-permute-start | bytes 27656 | tf_op jit(solution)/shard_map/ppermute | solution.py:25
  654.5 8.0 %collective-permute-start.75 = (f32[34,1,256]{2,1,0:T(1,128)S(1)}, f32[34,1,256]{2,1,0:T(1,128)S(1)}, u32[]{:S(2)}, u32[]{:S(2)}) collective-permute-start(f32[34,1,256]{2,1,0:T(1,128)S(1)} %get-tuple-element.61), channel_id=1, source_target_pairs={{1,0},{2,1},{3,2},{4,3},{5,4},{6,5},{7,6},{8,7},{9,8},{10,9},{11,1... | collective-permute-start | bytes 104456 | tf_op jit(solution)/shard_map/ppermute | solution.py:25
  673.5 8.0 %collective-permute-start.79 = (f32[34,1,256]{2,1,0:T(1,128)S(1)}, f32[34,1,256]{2,1,0:T(1,128)S(1)}, u32[]{:S(2)}, u32[]{:S(2)}) collective-permute-start(f32[34,1,256]{2,1,0:T(1,128)S(1)} %get-tuple-element.59), channel_id=1, source_target_pairs={{1,0},{2,1},{3,2},{4,3},{5,4},{6,5},{7,6},{8,7},{9,8},{10,9},{11,1... | collective-permute-start | bytes 104456 | tf_op jit(solution)/shard_map/ppermute | solution.py:25
  692.5 8.0 %collective-permute-start.83 = (f32[34,1,256]{2,1,0:T(1,128)S(1)}, f32[34,1,256]{2,1,0:T(1,128)S(1)}, u32[]{:S(2)}, u32[]{:S(2)}) collective-permute-start(f32[34,1,256]{2,1,0:T(1,128)S(1)} %get-tuple-element.57), channel_id=1, source_target_pairs={{1,0},{2,1},{3,2},{4,3},{5,4},{6,5},{7,6},{8,7},{9,8},{10,9},{11,1... | collective-permute-start | bytes 104456 | tf_op jit(solution)/shard_map/ppermute | solution.py:25
  (69 other events, 2280.3 us)
where the time goes:
time: 707 us; the launch traced here: 702 us
  starting transfers between devices  249 us (35%)
  local copies, waits for them, and re-layouts  146 us (21%)
  blocking collectives  117 us (17%)
  waiting for transfers between devices  98.8 us (14%)
  other arithmetic  88.2 us (12%)
    ppermute x42, starting transfers between devices, with_halo(): before = lax.ppermute(last, axis, up)  152 us
    ppermute x42, waiting for transfers between devices, with_halo(): after = lax.ppermute(leading, axis, down)  98.7 us
    ppermute x42, starting transfers between devices, with_halo(): after = lax.ppermute(leading, axis, down)  97.6 us
    reshape x4, local copies, waits for them, and re-layouts, restrict(): field.reshape(size_x // 2, 2, size_y // 2, 2, size_z // 2, 2)  79.5 us
    all_gather x1, blocking collectives, collect(): lax.all_gather(conduct, ('gx', 'gy'), axis=0, tiled=True)  59.7 us
    all_gather x1, blocking collectives, collect(): lax.all_gather(source, ('gx', 'gy'), axis=0, tiled=True)  57.4 us
    reduce_sum x10, other arithmetic, restrict(): jnp.mean(field.reshape(size_x // 2, 2, size_y // 2, 2, size_z // 2, 2), a...  38.5 us
    reshape x3, local copies, waits for them, and re-layouts, prolong(): return grown.reshape(2 * size_x, 2 * size_y, 2 * size_z)  29.9 us
  transfers between devices with their start and end apart: 84, of which 28 were waited for; matrix products, arithmetic and copies ran while one was open for 22% of the time, Pallas kernels for 0%

commit v1 on v0

--- a/solution.py
+++ b/solution.py
@@ -112,7 +112,10 @@
     count_x = lax.axis_size("gx")
     count_y = lax.axis_size("gy")
     gathered = (
-        lax.all_gather(source, ("gx", "gy"), axis=0, tiled=True),
+        jnp.concatenate(
+            lax.all_to_all(jnp.stack([source] * lax.axis_size(("gx", "gy"))), ("gx", "gy"), 0, 0),
+            axis=0,
+        ),
         lax.all_gather(conduct, ("gx", "gy"), axis=0, tiled=True),
     )
     arranged = []

time: 707 us -> 677 us (0.958)
  blocking collectives: 117 us -> 63.8 us
  starting transfers between devices: 249 us -> 264 us
  waiting for transfers between devices: 98.8 us -> 107 us
    all_gather x1 -> x0, blocking collectives: 57.4 us -> none  [collect(): lax.all_gather(source, ('gx', 'gy'), axis=0, tiled=True)]
    all_to_all x0 -> x1, starting transfers between devices: none -> 14 us  [collect(): lax.all_to_all(jnp.stack([source] * lax.axis_size(('gx', 'gy'))), ('gx',...]
    all_to_all x0 -> x1, waiting for transfers between devices: none -> 7.97 us  [collect(): lax.all_to_all(jnp.stack([source] * lax.axis_size(('gx', 'gy'))), ('gx',...]
  transfers between devices with their start and end apart: 84 -> 85, of which waited for: 28 -> 29; matrix products, arithmetic and copies ran while one was open for 22% -> 22% of each run, Pallas kernels for 0% -> 0%
where the time goes in v1:
time: 677 us; the launch traced here: 672 us
  starting transfers between devices  264 us (39%)
  local copies, waits for them, and re-layouts  151 us (22%)
  waiting for transfers between devices  107 us (16%)
  other arithmetic  83.1 us (12%)
  blocking collectives  63.8 us (9%)
    ppermute x42, starting transfers between devices, with_halo(): before = lax.ppermute(last, axis, up)  155 us
    ppermute x42, waiting for transfers between devices, with_halo(): after = lax.ppermute(leading, axis, down)  98.6 us
    ppermute x42, starting transfers between devices, with_halo(): after = lax.ppermute(leading, axis, down)  95.5 us
    reshape x4, local copies, waits for them, and re-layouts, restrict(): field.reshape(size_x // 2, 2, size_y // 2, 2, size_z // 2, 2)  78.9 us
    all_gather x1, blocking collectives, collect(): lax.all_gather(conduct, ('gx', 'gy'), axis=0, tiled=True)  63.8 us
    reduce_sum x10, other arithmetic, restrict(): jnp.mean(field.reshape(size_x // 2, 2, size_y // 2, 2, size_z // 2, 2), a...  37.9 us
    reshape x3, local copies, waits for them, and re-layouts, prolong(): return grown.reshape(2 * size_x, 2 * size_y, 2 * size_z)  29.9 us
    add x14, other arithmetic, chebyshev(): iterate = iterate + update  16.6 us
  transfers between devices with their start and end apart: 85, of which 29 were waited for; matrix products, arithmetic and copies ran while one was open for 22% of the time, Pallas kernels for 0%

profile of v1, /device:TPU:103, one launch (start us, length us, event | category | flops | bytes accessed | tf_op | source)
XLA Modules:
  0.0 671.7 jit_solution(14585589201160788660)
XLA Ops:
  1.4 3.8 collective-permute-start
  8.9 35.7 %reshape.74 = f32[16,2,8,2,128,2]{5,4,3,2,1,0:T(8,128)} reshape(f32[32,16,256]{2,1,0:T(8,128)} %param.3) | data formatting | bytes 1048576 | tf_op jit(solution)/shard_map/reshape | solution.py:93
  44.5 12.2 %reduce_sum.86 = f32[16,8,128]{2,1,0:T(8,128)S(1)} reduce(f32[16,2,8,2,128,2]{5,4,3,2,1,0:T(8,128)} %reshape.74, f32[]{:T(128)} %constant.35.clone.1), dimensions={1,3,5}, to_apply=%region_0.0 | reduce | flops 114688 | bytes 589828 | tf_op jit(solution)/shard_map/reduce_sum | solution.py:93
  56.9 4.7 collective-permute-start.2
  63.5 6.0 collective-permute-done.3
  71.5 5.1 collective-permute-start.4
  78.5 3.6 collective-permute-start.8
  90.2 5.5 div.201
  98.3 3.8 fusion.7
  102.1 4.2 collective-permute-start.12
  111.4 5.0 collective-permute-start.14
  118.4 6.7 collective-permute-start.10
  128.6 35.6 %reshape.75 = f32[16,2,8,2,128,2]{5,4,3,2,1,0:T(8,128)} reshape(f32[32,16,256]{2,1,0:T(8,128)} %fusion.13) | data formatting | bytes 1048576 | tf_op jit(solution)/shard_map/reshape | solution.py:93
  164.1 12.2 %reduce_sum.87 = f32[16,8,128]{2,1,0:T(8,128)S(1)} reduce(f32[16,2,8,2,128,2]{5,4,3,2,1,0:T(8,128)} %reshape.75, f32[]{:T(128)} %constant.35.clone.1), dimensions={1,3,5}, to_apply=%region_1.0 | reduce | flops 114688 | bytes 589828 | tf_op jit(solution)/shard_map/reduce_sum | solution.py:93
  184.8 3.6 collective-permute-start.20
  190.4 7.0 %collective-permute-start.18 = (f32[18,1,128]{2,1,0:T(1,128)S(1)}, f32[18,1,128]{2,1,0:T(1,128)S(1)}, u32[]{:S(2)}, u32[]{:S(2)}) collective-permute-start(f32[18,1,128]{2,1,0:T(1,128)S(1)} %get-tuple-element.88), channel_id=1, source_target_pairs={{0,1},{1,2},{2,3},{3,4},{4,5},{5,6},{6,7},{7,8},{8,9},{9,10},{10,1... | collective-permute-start | bytes 27656 | tf_op jit(solution)/shard_map/ppermute | solution.py:24
  206.6 5.1 collective-permute-start.24
  216.6 4.6 collective-permute-start.26
  224.6 6.7 collective-permute-start.22
  234.5 5.6 reshape.76
  249.3 3.6 collective-permute-start.32
  254.9 7.0 %collective-permute-start.30 = (f32[10,1,64]{2,1,0:T(1,128)S(1)}, f32[10,1,64]{2,1,0:T(1,128)S(1)}, u32[]{:S(2)}, u32[]{:S(2)}) collective-permute-start(f32[10,1,64]{2,1,0:T(1,128)S(1)} %get-tuple-element.110), channel_id=1, source_target_pairs={{0,1},{1,2},{2,3},{3,4},{4,5},{5,6},{6,7},{7,8},{8,9},{9,10},{10,1... | collective-permute-start | bytes 7688 | tf_op jit(solution)/shard_map/ppermute | solution.py:24
  265.2 4.3 collective-permute-done.31
  269.6 5.1 collective-permute-start.36
  285.5 5.2 collective-permute-start.34
  301.5 3.7 collective-permute-start.40
  310.9 4.3 collective-permute-start.42
  317.9 5.3 collective-permute-done.43
  324.8 4.5 collective-permute-start.44
  331.2 63.8 %all-gather.1 = f32[256,2,16]{2,1,0:T(2,128)} all-gather(f32[1,2,16]{2,1,0:T(2,128)S(1)} %multiply_bitcast_fusion), channel_id=2, replica_groups=mesh['gx'=8,'gy'=32] {'gx','gy'}, dimensions={0}, use_global_device_ids=true | all-gather | bytes 32896 | tf_op jit(solution)/shard_map/all_gather | solution.py:119
  396.9 4.4 collective-permute-start.46
  403.8 5.1 collective-permute-done.47
  414.7 14.0 %all-to-all-start = ((f32[256,2,1,16]{3,1,2,0:T(2,128)}), f32[256,2,1,16]{3,1,2,0:T(2,128)}, u32[]{:S(2)}, u32[]{:S(2)}) async-start(f32[256,2,1,16]{3,1,2,0:T(2,128)} %stack.2), calls=%async_computation | async-start | bytes 524288 | tf_op jit(solution)/shard_map/all_to_all | solution.py:116
  430.4 8.0 %all-to-all-done = f32[256,2,1,16]{3,1,2,0:T(2,128)} async-done(((f32[256,2,1,16]{3,1,2,0:T(2,128)}), f32[256,2,1,16]{3,1,2,0:T(2,128)}, u32[]{:S(2)}, u32[]{:S(2)}) %all-to-all-start) | async-done | bytes 32800 | tf_op jit(solution)/shard_map/all_to_all | solution.py:116
  460.4 3.9 collective-permute-start.50
  466.2 5.7 collective-permute-done.51
  486.3 4.3 collective-permute-done.55
  507.7 4.3 collective-permute-done.59
  522.9 3.6 collective-permute-start.63
  526.5 4.1 collective-permute-done.63
  534.1 4.0 reshape.82
  552.4 4.3 collective-permute-done.67
  571.2 4.3 collective-permute-done.71
  576.7 11.4 %broadcast_in_dim.36 = f32[16,2,8,2,128,2]{5,4,3,2,1,0:T(8,128)} broadcast(f32[16,8,128]{2,1,0:T(8,128)S(1)} %fusion.240), dimensions={0,2,4} | broadcast | bytes 589824 | tf_op jit(solution)/shard_map/broadcast_in_dim | solution.py:98
  588.2 24.6 %reshape.83 = f32[32,16,256]{2,1,0:T(8,128)} reshape(f32[16,2,8,2,128,2]{5,4,3,2,1,0:T(8,128)} %broadcast_in_dim.36) | data formatting | bytes 1048576 | tf_op jit(solution)/shard_map/reshape | solution.py:99
  627.6 4.6 collective-permute-done.75
  646.5 4.6 collective-permute-done.79
  665.5 4.6 collective-permute-done.83
  (318 shorter events, 265.9 us)
Async XLA Ops:
  1.4 55.4 %collective-permute-start = (f32[1,16,256]{2,1,0:T(8,128)S(1)}, f32[1,16,256]{2,1,0:T(8,128)S(1)}, u32[]{:S(2)}, u32[]{:S(2)}) collective-permute-start(f32[1,16,256]{2,1,0:T(8,128)S(1)} %get-tuple-element.79), channel_id=1, source_target_pairs={{0,32},{32,64},{64,96},{96,128},{128,160},{160,192},{192,224},{1,3... | collective-permute-start | bytes 49160 | tf_op jit(solution)/shard_map/ppermute | solution.py:24
  5.1 51.7 %collective-permute-start.1 = (f32[1,16,256]{2,1,0:T(8,128)S(1)}, f32[1,16,256]{2,1,0:T(8,128)S(1)}, u32[]{:S(2)}, u32[]{:S(2)}) collective-permute-start(f32[1,16,256]{2,1,0:T(8,128)S(1)} %get-tuple-element.78), channel_id=1, source_target_pairs={{32,0},{64,32},{96,64},{128,96},{160,128},{192,160},{224,192},{33,... | collective-permute-start | bytes 49160 | tf_op jit(solution)/shard_map/ppermute | solution.py:25
  61.6 8.0 %collective-permute-start.3 = (f32[34,1,256]{2,1,0:T(1,128)S(1)}, f32[34,1,256]{2,1,0:T(1,128)S(1)}, u32[]{:S(2)}, u32[]{:S(2)}) collective-permute-start(f32[34,1,256]{2,1,0:T(1,128)S(1)} %get-tuple-element.64), channel_id=1, source_target_pairs={{1,0},{2,1},{3,2},{4,3},{5,4},{6,5},{7,6},{8,7},{9,8},{10,9},{11,1... | collective-permute-start | bytes 104456 | tf_op jit(solution)/shard_map/ppermute | solution.py:25
  71.5 12.6 %collective-permute-start.4 = (f32[1,16,256]{2,1,0:T(8,128)S(1)}, f32[1,16,256]{2,1,0:T(8,128)S(1)}, u32[]{:S(2)}, u32[]{:S(2)}) collective-permute-start(f32[1,16,256]{2,1,0:T(8,128)S(1)} %get-tuple-element.74), channel_id=1, source_target_pairs={{0,32},{32,64},{64,96},{96,128},{128,160},{160,192},{192,224},{1,3... | collective-permute-start | bytes 49160 | tf_op jit(solution)/shard_map/ppermute | solution.py:24
  78.5 39.8 %collective-permute-start.8 = (f32[1,8,128]{2,1,0:T(8,128)S(1)}, f32[1,8,128]{2,1,0:T(8,128)S(1)}, u32[]{:S(2)}, u32[]{:S(2)}) collective-permute-start(f32[1,8,128]{2,1,0:T(8,128)S(1)} %get-tuple-element.102), channel_id=1, source_target_pairs={{0,32},{32,64},{64,96},{96,128},{128,160},{160,192},{192,224},{1,3... | collective-permute-start | bytes 12296 | tf_op jit(solution)/shard_map/ppermute | solution.py:24
  82.1 36.2 %collective-permute-start.9 = (f32[1,8,128]{2,1,0:T(8,128)S(1)}, f32[1,8,128]{2,1,0:T(8,128)S(1)}, u32[]{:S(2)}, u32[]{:S(2)}) collective-permute-start(f32[1,8,128]{2,1,0:T(8,128)S(1)} %get-tuple-element.103), channel_id=1, source_target_pairs={{32,0},{64,32},{96,64},{128,96},{160,128},{192,160},{224,192},{33,... | collective-permute-start | bytes 12296 | tf_op jit(solution)/shard_map/ppermute | solution.py:25
  84.2 14.1 %collective-permute-start.6 = (f32[34,1,256]{2,1,0:T(1,128)S(1)}, f32[34,1,256]{2,1,0:T(1,128)S(1)}, u32[]{:S(2)}, u32[]{:S(2)}) collective-permute-start(f32[34,1,256]{2,1,0:T(1,128)S(1)} %get-tuple-element.62), channel_id=1, source_target_pairs={{0,1},{1,2},{2,3},{3,4},{4,5},{5,6},{6,7},{7,8},{8,9},{9,10},{10,1... | collective-permute-start | bytes 104456 | tf_op jit(solution)/shard_map/ppermute | solution.py:24
  86.1 12.2 %collective-permute-start.7 = (f32[34,1,256]{2,1,0:T(1,128)S(1)}, f32[34,1,256]{2,1,0:T(1,128)S(1)}, u32[]{:S(2)}, u32[]{:S(2)}) collective-permute-start(f32[34,1,256]{2,1,0:T(1,128)S(1)} %get-tuple-element.63), channel_id=1, source_target_pairs={{1,0},{2,1},{3,2},{4,3},{5,4},{6,5},{7,6},{8,7},{9,8},{10,9},{11,1... | collective-permute-start | bytes 104456 | tf_op jit(solution)/shard_map/ppermute | solution.py:25
  111.4 15.6 %collective-permute-start.14 = (f32[34,1,256]{2,1,0:T(1,128)S(1)}, f32[34,1,256]{2,1,0:T(1,128)S(1)}, u32[]{:S(2)}, u32[]{:S(2)}) collective-permute-start(f32[34,1,256]{2,1,0:T(1,128)S(1)} %get-tuple-element.60), channel_id=1, source_target_pairs={{0,1},{1,2},{2,3},{3,4},{4,5},{5,6},{6,7},{7,8},{8,9},{9,10},{10,1... | collective-permute-start | bytes 104456 | tf_op jit(solution)/shard_map/ppermute | solution.py:24
  116.4 10.6 %collective-permute-start.15 = (f32[34,1,256]{2,1,0:T(1,128)S(1)}, f32[34,1,256]{2,1,0:T(1,128)S(1)}, u32[]{:S(2)}, u32[]{:S(2)}) collective-permute-start(f32[34,1,256]{2,1,0:T(1,128)S(1)} %get-tuple-element.61), channel_id=1, source_target_pairs={{1,0},{2,1},{3,2},{4,3},{5,4},{6,5},{7,6},{8,7},{9,8},{10,9},{11,1... | collective-permute-start | bytes 104456 | tf_op jit(solution)/shard_map/ppermute | solution.py:25
  118.4 58.0 %collective-permute-start.10 = (f32[18,1,128]{2,1,0:T(1,128)S(1)}, f32[18,1,128]{2,1,0:T(1,128)S(1)}, u32[]{:S(2)}, u32[]{:S(2)}) collective-permute-start(f32[18,1,128]{2,1,0:T(1,128)S(1)} %get-tuple-element.91), channel_id=1, source_target_pairs={{0,1},{1,2},{2,3},{3,4},{4,5},{5,6},{6,7},{7,8},{8,9},{9,10},{10,1... | collective-permute-start | bytes 27656 | tf_op jit(solution)/shard_map/ppermute | solution.py:24
  125.1 51.3 %collective-permute-start.11 = (f32[18,1,128]{2,1,0:T(1,128)S(1)}, f32[18,1,128]{2,1,0:T(1,128)S(1)}, u32[]{:S(2)}, u32[]{:S(2)}) collective-permute-start(f32[18,1,128]{2,1,0:T(1,128)S(1)} %get-tuple-element.90), channel_id=1, source_target_pairs={{1,0},{2,1},{3,2},{4,3},{5,4},{6,5},{7,6},{8,7},{9,8},{10,9},{11,1... | collective-permute-start | bytes 27656 | tf_op jit(solution)/shard_map/ppermute | solution.py:25
  178.8 11.6 %collective-permute-start.16 = (f32[1,8,128]{2,1,0:T(8,128)S(1)}, f32[1,8,128]{2,1,0:T(8,128)S(1)}, u32[]{:S(2)}, u32[]{:S(2)}) collective-permute-start(f32[1,8,128]{2,1,0:T(8,128)S(1)} %get-tuple-element.98), channel_id=1, source_target_pairs={{0,32},{32,64},{64,96},{96,128},{128,160},{160,192},{192,224},{1,3... | collective-permute-start | bytes 12296 | tf_op jit(solution)/shard_map/ppermute | solution.py:24
  181.6 8.8 %collective-permute-start.17 = (f32[1,8,128]{2,1,0:T(8,128)S(1)}, f32[1,8,128]{2,1,0:T(8,128)S(1)}, u32[]{:S(2)}, u32[]{:S(2)}) collective-permute-start(f32[1,8,128]{2,1,0:T(8,128)S(1)} %get-tuple-element.99), channel_id=1, source_target_pairs={{32,0},{64,32},{96,64},{128,96},{160,128},{192,160},{224,192},{33,... | collective-permute-start | bytes 12296 | tf_op jit(solution)/shard_map/ppermute | solution.py:25
  184.8 38.4 %collective-permute-start.20 = (f32[1,4,64]{2,1,0:T(4,128)}, f32[1,4,64]{2,1,0:T(4,128)S(1)}, u32[]{:S(2)}, u32[]{:S(2)}) collective-permute-start(f32[1,4,64]{2,1,0:T(4,128)} %get-tuple-element.124), channel_id=1, source_target_pairs={{0,32},{32,64},{64,96},{96,128},{128,160},{160,192},{192,224},{1,3... | collective-permute-start | bytes 3080 | tf_op jit(solution)/shard_map/ppermute | solution.py:24
  188.4 34.8 %collective-permute-start.21 = (f32[1,4,64]{2,1,0:T(4,128)}, f32[1,4,64]{2,1,0:T(4,128)}, u32[]{:S(2)}, u32[]{:S(2)}) collective-permute-start(f32[1,4,64]{2,1,0:T(4,128)} %get-tuple-element.125), channel_id=1, source_target_pairs={{32,0},{64,32},{96,64},{128,96},{160,128},{192,160},{224,192},{33,... | collective-permute-start | bytes 3080 | tf_op jit(solution)/shard_map/ppermute | solution.py:25
  190.4 13.6 %collective-permute-start.18 = (f32[18,1,128]{2,1,0:T(1,128)S(1)}, f32[18,1,128]{2,1,0:T(1,128)S(1)}, u32[]{:S(2)}, u32[]{:S(2)}) collective-permute-start(f32[18,1,128]{2,1,0:T(1,128)S(1)} %get-tuple-element.88), channel_id=1, source_target_pairs={{0,1},{1,2},{2,3},{3,4},{4,5},{5,6},{6,7},{7,8},{8,9},{9,10},{10,1... | collective-permute-start | bytes 27656 | tf_op jit(solution)/shard_map/ppermute | solution.py:24
  197.4 7.8 %collective-permute-start.19 = (f32[18,1,128]{2,1,0:T(1,128)S(1)}, f32[18,1,128]{2,1,0:T(1,128)}, u32[]{:S(2)}, u32[]{:S(2)}) collective-permute-start(f32[18,1,128]{2,1,0:T(1,128)S(1)} %get-tuple-element.89), channel_id=1, source_target_pairs={{1,0},{2,1},{3,2},{4,3},{5,4},{6,5},{7,6},{8,7},{9,8},{10,9},{11,1... | collective-permute-start | bytes 27656 | tf_op jit(solution)/shard_map/ppermute | solution.py:25
  206.6 8.2 %collective-permute-start.24 = (f32[1,8,128]{2,1,0:T(8,128)S(1)}, f32[1,8,128]{2,1,0:T(8,128)S(1)}, u32[]{:S(2)}, u32[]{:S(2)}) collective-permute-start(f32[1,8,128]{2,1,0:T(8,128)S(1)} %get-tuple-element.96), channel_id=1, source_target_pairs={{0,32},{32,64},{64,96},{96,128},{128,160},{160,192},{192,224},{1,3... | collective-permute-start | bytes 12296 | tf_op jit(solution)/shard_map/ppermute | solution.py:24
  216.6 16.8 %collective-permute-start.26 = (f32[18,1,128]{2,1,0:T(1,128)S(1)}, f32[18,1,128]{2,1,0:T(1,128)S(1)}, u32[]{:S(2)}, u32[]{:S(2)}) collective-permute-start(f32[18,1,128]{2,1,0:T(1,128)S(1)} %get-tuple-element.86), channel_id=1, source_target_pairs={{0,1},{1,2},{2,3},{3,4},{4,5},{5,6},{6,7},{7,8},{8,9},{9,10},{10,1... | collective-permute-start | bytes 27656 | tf_op jit(solution)/shard_map/ppermute | solution.py:24
  221.3 12.2 %collective-permute-start.27 = (f32[18,1,128]{2,1,0:T(1,128)S(1)}, f32[18,1,128]{2,1,0:T(1,128)S(1)}, u32[]{:S(2)}, u32[]{:S(2)}) collective-permute-start(f32[18,1,128]{2,1,0:T(1,128)S(1)} %get-tuple-element.87), channel_id=1, source_target_pairs={{1,0},{2,1},{3,2},{4,3},{5,4},{6,5},{7,6},{8,7},{9,8},{10,9},{11,1... | collective-permute-start | bytes 27656 | tf_op jit(solution)/shard_map/ppermute | solution.py:25
  224.6 18.0 %collective-permute-start.22 = (f32[10,1,64]{2,1,0:T(1,128)}, f32[10,1,64]{2,1,0:T(1,128)}, u32[]{:S(2)}, u32[]{:S(2)}) collective-permute-start(f32[10,1,64]{2,1,0:T(1,128)} %get-tuple-element.113), channel_id=1, source_target_pairs={{0,1},{1,2},{2,3},{3,4},{4,5},{5,6},{6,7},{7,8},{8,9},{9,10},{10,1... | collective-permute-start | bytes 7688 | tf_op jit(solution)/shard_map/ppermute | solution.py:24
  231.3 11.3 %collective-permute-start.23 = (f32[10,1,64]{2,1,0:T(1,128)}, f32[10,1,64]{2,1,0:T(1,128)}, u32[]{:S(2)}, u32[]{:S(2)}) collective-permute-start(f32[10,1,64]{2,1,0:T(1,128)} %get-tuple-element.112), channel_id=1, source_target_pairs={{1,0},{2,1},{3,2},{4,3},{5,4},{6,5},{7,6},{8,7},{9,8},{10,9},{11,1... | collective-permute-start | bytes 7688 | tf_op jit(solution)/shard_map/ppermute | solution.py:25
  243.8 11.1 %collective-permute-start.28 = (f32[1,4,64]{2,1,0:T(4,128)S(1)}, f32[1,4,64]{2,1,0:T(4,128)S(1)}, u32[]{:S(2)}, u32[]{:S(2)}) collective-permute-start(f32[1,4,64]{2,1,0:T(4,128)S(1)} %get-tuple-element.120), channel_id=1, source_target_pairs={{0,32},{32,64},{64,96},{96,128},{128,160},{160,192},{192,224},{1,3... | collective-permute-start | bytes 3080 | tf_op jit(solution)/shard_map/ppermute | solution.py:24
  246.6 8.3 %collective-permute-start.29 = (f32[1,4,64]{2,1,0:T(4,128)S(1)}, f32[1,4,64]{2,1,0:T(4,128)S(1)}, u32[]{:S(2)}, u32[]{:S(2)}) collective-permute-start(f32[1,4,64]{2,1,0:T(4,128)S(1)} %get-tuple-element.121), channel_id=1, source_target_pairs={{32,0},{64,32},{96,64},{128,96},{160,128},{192,160},{224,192},{33,... | collective-permute-start | bytes 3080 | tf_op jit(solution)/shard_map/ppermute | solution.py:25
  249.3 27.4 %collective-permute-start.32 = (f32[1,2,32]{2,0,1:T(1,128)S(1)}, f32[1,2,32]{2,0,1:T(1,128)S(1)}, u32[]{:S(2)}, u32[]{:S(2)}) collective-permute-start(f32[1,2,32]{2,0,1:T(1,128)S(1)} %get-tuple-element.148), channel_id=1, source_target_pairs={{0,32},{32,64},{64,96},{96,128},{128,160},{160,192},{192,224},{1,3... | collective-permute-start | bytes 776 | tf_op jit(solution)/shard_map/ppermute | solution.py:24
  252.9 23.8 %collective-permute-start.33 = (f32[1,2,32]{2,0,1:T(1,128)S(1)}, f32[1,2,32]{2,0,1:T(1,128)S(1)}, u32[]{:S(2)}, u32[]{:S(2)}) collective-permute-start(f32[1,2,32]{2,0,1:T(1,128)S(1)} %get-tuple-element.149), channel_id=1, source_target_pairs={{32,0},{64,32},{96,64},{128,96},{160,128},{192,160},{224,192},{33,... | collective-permute-start | bytes 776 | tf_op jit(solution)/shard_map/ppermute | solution.py:25
  254.9 10.3 %collective-permute-start.30 = (f32[10,1,64]{2,1,0:T(1,128)S(1)}, f32[10,1,64]{2,1,0:T(1,128)S(1)}, u32[]{:S(2)}, u32[]{:S(2)}) collective-permute-start(f32[10,1,64]{2,1,0:T(1,128)S(1)} %get-tuple-element.110), channel_id=1, source_target_pairs={{0,1},{1,2},{2,3},{3,4},{4,5},{5,6},{6,7},{7,8},{8,9},{9,10},{10,1... | collective-permute-start | bytes 7688 | tf_op jit(solution)/shard_map/ppermute | solution.py:24
  261.8 7.7 %collective-permute-start.31 = (f32[10,1,64]{2,1,0:T(1,128)S(1)}, f32[10,1,64]{2,1,0:T(1,128)S(1)}, u32[]{:S(2)}, u32[]{:S(2)}) collective-permute-start(f32[10,1,64]{2,1,0:T(1,128)S(1)} %get-tuple-element.111), channel_id=1, source_target_pairs={{1,0},{2,1},{3,2},{4,3},{5,4},{6,5},{7,6},{8,7},{9,8},{10,9},{11,1... | collective-permute-start | bytes 7688 | tf_op jit(solution)/shard_map/ppermute | solution.py:25
  269.6 7.7 %collective-permute-start.36 = (f32[1,4,64]{2,1,0:T(4,128)S(1)}, f32[1,4,64]{2,1,0:T(4,128)S(1)}, u32[]{:S(2)}, u32[]{:S(2)}) collective-permute-start(f32[1,4,64]{2,1,0:T(4,128)S(1)} %get-tuple-element.118), channel_id=1, source_target_pairs={{0,32},{32,64},{64,96},{96,128},{128,160},{160,192},{192,224},{1,3... | collective-permute-start | bytes 3080 | tf_op jit(solution)/shard_map/ppermute | solution.py:24
  279.6 13.1 %collective-permute-start.38 = (f32[10,1,64]{2,1,0:T(1,128)S(1)}, f32[10,1,64]{2,1,0:T(1,128)S(1)}, u32[]{:S(2)}, u32[]{:S(2)}) collective-permute-start(f32[10,1,64]{2,1,0:T(1,128)S(1)} %get-tuple-element.108), channel_id=1, source_target_pairs={{0,1},{1,2},{2,3},{3,4},{4,5},{5,6},{6,7},{7,8},{8,9},{9,10},{10,1... | collective-permute-start | bytes 7688 | tf_op jit(solution)/shard_map/ppermute | solution.py:24
  281.6 11.1 %collective-permute-start.39 = (f32[10,1,64]{2,1,0:T(1,128)S(1)}, f32[10,1,64]{2,1,0:T(1,128)S(1)}, u32[]{:S(2)}, u32[]{:S(2)}) collective-permute-start(f32[10,1,64]{2,1,0:T(1,128)S(1)} %get-tuple-element.109), channel_id=1, source_target_pairs={{1,0},{2,1},{3,2},{4,3},{5,4},{6,5},{7,6},{8,7},{9,8},{10,9},{11,1... | collective-permute-start | bytes 7688 | tf_op jit(solution)/shard_map/ppermute | solution.py:25
  285.5 11.7 %collective-permute-start.34 = (f32[6,1,32]{2,0,1:T(8,128)}, f32[6,1,32]{2,0,1:T(8,128)}, u32[]{:S(2)}, u32[]{:S(2)}) collective-permute-start(f32[6,1,32]{2,0,1:T(8,128)} %get-tuple-element.135), channel_id=1, source_target_pairs={{0,1},{1,2},{2,3},{3,4},{4,5},{5,6},{6,7},{7,8},{8,9},{9,10},{10,1... | collective-permute-start | bytes 2312 | tf_op jit(solution)/shard_map/ppermute | solution.py:24
  290.8 8.0 %collective-permute-start.35 = (f32[6,1,32]{2,0,1:T(8,128)}, f32[6,1,32]{2,0,1:T(8,128)}, u32[]{:S(2)}, u32[]{:S(2)}) collective-permute-start(f32[6,1,32]{2,0,1:T(8,128)} %get-tuple-element.134), channel_id=1, source_target_pairs={{1,0},{2,1},{3,2},{4,3},{5,4},{6,5},{7,6},{8,7},{9,8},{10,9},{11,1... | collective-permute-start | bytes 2312 | tf_op jit(solution)/shard_map/ppermute | solution.py:25
  301.5 8.4 %collective-permute-start.40 = (f32[1,2,32]{2,0,1:T(1,128)}, f32[1,2,32]{2,0,1:T(1,128)}, u32[]{:S(2)}, u32[]{:S(2)}) collective-permute-start(f32[1,2,32]{2,0,1:T(1,128)} %get-tuple-element.144), channel_id=1, source_target_pairs={{0,32},{32,64},{64,96},{96,128},{128,160},{160,192},{192,224},{1,3... | collective-permute-start | bytes 776 | tf_op jit(solution)/shard_map/ppermute | solution.py:24
  315.3 7.9 %collective-permute-start.43 = (f32[6,1,32]{2,0,1:T(8,128)S(1)}, f32[6,1,32]{2,0,1:T(8,128)S(1)}, u32[]{:S(2)}, u32[]{:S(2)}) collective-permute-start(f32[6,1,32]{2,0,1:T(8,128)S(1)} %get-tuple-element.133), channel_id=1, source_target_pairs={{1,0},{2,1},{3,2},{4,3},{5,4},{6,5},{7,6},{8,7},{9,8},{10,9},{11,1... | collective-permute-start | bytes 2312 | tf_op jit(solution)/shard_map/ppermute | solution.py:25
  324.8 71.4 %collective-permute-start.44 = (f32[1,2,32]{2,0,1:T(1,128)}, f32[1,2,32]{2,0,1:T(1,128)}, u32[]{:S(2)}, u32[]{:S(2)}) collective-permute-start(f32[1,2,32]{2,0,1:T(1,128)} %get-tuple-element.140), channel_id=1, source_target_pairs={{0,32},{32,64},{64,96},{96,128},{128,160},{160,192},{192,224},{1,3... | collective-permute-start | bytes 776 | tf_op jit(solution)/shard_map/ppermute | solution.py:24
  329.2 66.9 %collective-permute-start.45 = (f32[1,2,32]{2,0,1:T(1,128)}, f32[1,2,32]{2,0,1:T(1,128)}, u32[]{:S(2)}, u32[]{:S(2)}) collective-permute-start(f32[1,2,32]{2,0,1:T(1,128)} %get-tuple-element.141), channel_id=1, source_target_pairs={{32,0},{64,32},{96,64},{128,96},{160,128},{192,160},{224,192},{33,... | collective-permute-start | bytes 776 | tf_op jit(solution)/shard_map/ppermute | solution.py:25
  401.2 7.7 %collective-permute-start.47 = (f32[6,1,32]{2,0,1:T(8,128)S(1)}, f32[6,1,32]{2,0,1:T(8,128)S(1)}, u32[]{:S(2)}, u32[]{:S(2)}) collective-permute-start(f32[6,1,32]{2,0,1:T(8,128)S(1)} %get-tuple-element.131), channel_id=1, source_target_pairs={{1,0},{2,1},{3,2},{4,3},{5,4},{6,5},{7,6},{8,7},{9,8},{10,9},{11,1... | collective-permute-start | bytes 2312 | tf_op jit(solution)/shard_map/ppermute | solution.py:25
  414.7 23.7 %all-to-all-start = ((f32[256,2,1,16]{3,1,2,0:T(2,128)}), f32[256,2,1,16]{3,1,2,0:T(2,128)}, u32[]{:S(2)}, u32[]{:S(2)}) async-start(f32[256,2,1,16]{3,1,2,0:T(2,128)} %stack.2), calls=%async_computation | async-start | bytes 524288 | tf_op jit(solution)/shard_map/all_to_all | solution.py:116
  464.3 7.7 %collective-permute-start.51 = (f32[6,1,32]{2,0,1:T(8,128)S(1)}, f32[6,1,32]{2,0,1:T(8,128)S(1)}, u32[]{:S(2)}, u32[]{:S(2)}) collective-permute-start(f32[6,1,32]{2,0,1:T(8,128)S(1)} %get-tuple-element.129), channel_id=1, source_target_pairs={{1,0},{2,1},{3,2},{4,3},{5,4},{6,5},{7,6},{8,7},{9,8},{10,9},{11,1... | collective-permute-start | bytes 2312 | tf_op jit(solution)/shard_map/ppermute | solution.py:25
  504.3 7.7 %collective-permute-start.59 = (f32[10,1,64]{2,1,0:T(1,128)S(1)}, f32[10,1,64]{2,1,0:T(1,128)S(1)}, u32[]{:S(2)}, u32[]{:S(2)}) collective-permute-start(f32[10,1,64]{2,1,0:T(1,128)S(1)} %get-tuple-element.107), channel_id=1, source_target_pairs={{1,0},{2,1},{3,2},{4,3},{5,4},{6,5},{7,6},{8,7},{9,8},{10,9},{11,1... | collective-permute-start | bytes 7688 | tf_op jit(solution)/shard_map/ppermute | solution.py:25
  522.9 7.7 %collective-permute-start.63 = (f32[10,1,64]{2,1,0:T(1,128)S(1)}, f32[10,1,64]{2,1,0:T(1,128)S(1)}, u32[]{:S(2)}, u32[]{:S(2)}) collective-permute-start(f32[10,1,64]{2,1,0:T(1,128)S(1)} %get-tuple-element.105), channel_id=1, source_target_pairs={{1,0},{2,1},{3,2},{4,3},{5,4},{6,5},{7,6},{8,7},{9,8},{10,9},{11,1... | collective-permute-start | bytes 7688 | tf_op jit(solution)/shard_map/ppermute | solution.py:25
  549.0 7.7 %collective-permute-start.67 = (f32[18,1,128]{2,1,0:T(1,128)S(1)}, f32[18,1,128]{2,1,0:T(1,128)S(1)}, u32[]{:S(2)}, u32[]{:S(2)}) collective-permute-start(f32[18,1,128]{2,1,0:T(1,128)S(1)} %get-tuple-element.85), channel_id=1, source_target_pairs={{1,0},{2,1},{3,2},{4,3},{5,4},{6,5},{7,6},{8,7},{9,8},{10,9},{11,1... | collective-permute-start | bytes 27656 | tf_op jit(solution)/shard_map/ppermute | solution.py:25
  567.9 7.7 %collective-permute-start.71 = (f32[18,1,128]{2,1,0:T(1,128)S(1)}, f32[18,1,128]{2,1,0:T(1,128)S(1)}, u32[]{:S(2)}, u32[]{:S(2)}) collective-permute-start(f32[18,1,128]{2,1,0:T(1,128)S(1)} %get-tuple-element.83), channel_id=1, source_target_pairs={{1,0},{2,1},{3,2},{4,3},{5,4},{6,5},{7,6},{8,7},{9,8},{10,9},{11,1... | collective-permute-start | bytes 27656 | tf_op jit(solution)/shard_map/ppermute | solution.py:25
  624.2 8.0 %collective-permute-start.75 = (f32[34,1,256]{2,1,0:T(1,128)S(1)}, f32[34,1,256]{2,1,0:T(1,128)S(1)}, u32[]{:S(2)}, u32[]{:S(2)}) collective-permute-start(f32[34,1,256]{2,1,0:T(1,128)S(1)} %get-tuple-element.59), channel_id=1, source_target_pairs={{1,0},{2,1},{3,2},{4,3},{5,4},{6,5},{7,6},{8,7},{9,8},{10,9},{11,1... | collective-permute-start | bytes 104456 | tf_op jit(solution)/shard_map/ppermute | solution.py:25
  643.1 8.0 %collective-permute-start.79 = (f32[34,1,256]{2,1,0:T(1,128)S(1)}, f32[34,1,256]{2,1,0:T(1,128)S(1)}, u32[]{:S(2)}, u32[]{:S(2)}) collective-permute-start(f32[34,1,256]{2,1,0:T(1,128)S(1)} %get-tuple-element.57), channel_id=1, source_target_pairs={{1,0},{2,1},{3,2},{4,3},{5,4},{6,5},{7,6},{8,7},{9,8},{10,9},{11,1... | collective-permute-start | bytes 104456 | tf_op jit(solution)/shard_map/ppermute | solution.py:25
  662.1 8.0 %collective-permute-start.83 = (f32[34,1,256]{2,1,0:T(1,128)S(1)}, f32[34,1,256]{2,1,0:T(1,128)S(1)}, u32[]{:S(2)}, u32[]{:S(2)}) collective-permute-start(f32[34,1,256]{2,1,0:T(1,128)S(1)} %get-tuple-element.55), channel_id=1, source_target_pairs={{1,0},{2,1},{3,2},{4,3},{5,4},{6,5},{7,6},{8,7},{9,8},{10,9},{11,1... | collective-permute-start | bytes 104456 | tf_op jit(solution)/shard_map/ppermute | solution.py:25
  (71 other events, 2896.8 us)
